TPU v7x, 32 devices: a whole 2x2x4 slice. The times are simulated.
32 devices in a mesh: groups: 2 (over y), rows: 16 (over z, x, core), cols: 1.
Axes of the slice: x: 2, y: 2, z: 4, core: 2. Of those that a mesh axis runs over, the one named last changes fastest.
Arguments:
- pair_in: bfloat16 [256, 128, 128], P(('groups', 'rows'), 'cols'), parts along dimension 0, may hold values from -6 to 450
- single_in: float32 [256, 384], P(('groups', 'rows')), parts along dimension 0, may hold values from -6 to 6
- frames_in: float32 [12, 256], P(None, ('groups', 'rows')), parts along dimension 1, may hold values from -3 to 3, as said below
- dist_bins: int32 [2, 256, 128], P(None, ('groups', 'rows'), 'cols'), parts along dimension 1, may hold values from 0 to 14
- res_mask: int32 [256], P('groups'), parts along dimension 0, may hold values from 0 to 1, as said below
- chain_ids: int32 [256], P('groups'), parts along dimension 0, may hold values from 0 to 7, never falling along the last dimension, each value on 1 to 32 neighbouring positions
- w_left: bfloat16 [384, 128], replicated, may hold values from -0.3125 to 0.3125
- w_right: bfloat16 [384, 128], replicated, may hold values from -0.3125 to 0.3125
- dist_embed: bfloat16 [15, 128], replicated, may hold values from -6 to 6
- chain_embed: bfloat16 [2, 128], replicated, may hold values from -6 to 6
- pair_gain: float32 [128], replicated, may hold values from 0.5 to 1.5
- mlp_in: bfloat16 [128, 512], replicated, may hold values from -0.5 to 0.5
- mlp_bias: float32 [512], replicated, may hold values from -3 to 3
- mlp_out: bfloat16 [512, 128], replicated, may hold values from -0.25 to 0.25
- w_qkv: bfloat16 [384, 576], replicated, may hold values from -0.3125 to 0.3125
- w_points: bfloat16 [384, 576], replicated, may hold values from -0.3125 to 0.3125
- bias_weight: bfloat16 [128, 12], replicated, may hold values from -0.5 to 0.5
- point_scale: float32 [12], replicated, may hold values from 0.3 to 3
- w_out: bfloat16 [2112, 384], replicated, may hold values from -0.125 to 0.125
- single_gain: float32 [384], replicated, may hold values from 0.5 to 1.5
- w_frame: bfloat16 [384, 6], replicated, may hold values from -0.3125 to 0.3125
Outputs:
- pair_out: bfloat16 [256, 128, 128], P(('groups', 'rows'), 'cols'), parts along dimension 0
- single_out: float32 [256, 384], P(('groups', 'rows')), parts along dimension 0
- frames_out: float32 [12, 256], P(None, ('groups', 'rows')), parts along dimension 1
There are 2 independent parts, one for each index of `groups`. A program takes and returns all parts, laid end to end along the dimension named above; an argument that names none is the same for every part. Nothing has to cross between parts.
Inputs may be any that keep to these rules, and one draw needn't show every extreme that they name: `frames_in`: column n holds a rotation matrix in rows 0 to 8 (row-major) and a translation in rows 9 to 11. `res_mask`: 1 on a prefix of the residues, at least 64 and at most 127 of them. `chain_ids`: never falling along the residues; a chain holds 1 to 32 residues.
All inputs are finite; a program needn't handle non-finite values.
Results may differ from a plain program's by a relative error of at most 0.022.
Values may be sent and summed in bfloat16 or wider, within the bound.
A program may use at most 64 MiB of HBM per device.

v0:
```python
import math
import jax
import jax.numpy as jnp
from jax import lax
from jax.sharding import PartitionSpec as P

NQP = 4
CYCLES = 2
HIGHEST = lax.Precision.HIGHEST


def layer_norm(values, norm_gain):
    centre = jnp.mean(values, axis=-1, keepdims=True)
    spread = values - centre
    second = jnp.mean(spread * spread, axis=-1, keepdims=True)
    return spread * lax.rsqrt(second + 1e-05) * norm_gain


def to_global(points, frames):
    turns = frames[:, :9].reshape(-1, 3, 3)
    return jnp.einsum("nab,nbx->nax", turns, points, precision=HIGHEST) + frames[:, 9:12, None]


def to_local(points, frames):
    turns = frames[:, :9].reshape(-1, 3, 3)
    return jnp.einsum("nab,nax->nbx", turns, points - frames[:, 9:12, None], precision=HIGHEST)


def update_frames(frames, frame_step):
    quat_scale = lax.rsqrt(1.0 + jnp.sum(frame_step[:, :3] * frame_step[:, :3], axis=1))
    quat_b = frame_step[:, 0] * quat_scale
    quat_c = frame_step[:, 1] * quat_scale
    quat_d = frame_step[:, 2] * quat_scale
    entries = [
        quat_scale * quat_scale + quat_b * quat_b - quat_c * quat_c - quat_d * quat_d,
        2.0 * (quat_b * quat_c - quat_scale * quat_d),
        2.0 * (quat_b * quat_d + quat_scale * quat_c),
        2.0 * (quat_b * quat_c + quat_scale * quat_d),
        quat_scale * quat_scale - quat_b * quat_b + quat_c * quat_c - quat_d * quat_d,
        2.0 * (quat_c * quat_d - quat_scale * quat_b),
        2.0 * (quat_b * quat_d - quat_scale * quat_c),
        2.0 * (quat_c * quat_d + quat_scale * quat_b),
        quat_scale * quat_scale - quat_b * quat_b - quat_c * quat_c + quat_d * quat_d,
    ]
    turn_matrix = jnp.stack(entries, axis=1).reshape(-1, 3, 3)
    before = frames[:, :9].reshape(-1, 3, 3)
    rotated = jnp.einsum("nab,nbc->nac", before, turn_matrix, precision=HIGHEST)
    new_shift = (
        jnp.einsum("nab,nb->na", before, frame_step[:, 3:6], precision=HIGHEST) + frames[:, 9:12]
    )
    return jnp.concatenate([rotated.reshape(-1, 9), new_shift], axis=1)


def update_row(
    pair_row,
    bins_row,
    left_row,
    mask_row,
    same_row,
    right_keys,
    dist_embed,
    chain_embed,
    pair_gain,
    mlp_in,
    mlp_bias,
    mlp_out,
):
    onehot = (
        bins_row[:, None] == jnp.arange(dist_embed.shape[0], dtype=jnp.int32)[None, :]
    ).astype(jnp.bfloat16)
    looked = jnp.dot(onehot, dist_embed, preferred_element_type=jnp.float32)
    chain_part = jnp.where(
        same_row[:, None], chain_embed[1].astype(jnp.float32), chain_embed[0].astype(jnp.float32)
    )
    summed = (
        pair_row.astype(jnp.float32)
        + mask_row[:, None] * (left_row[None, :] + right_keys.astype(jnp.float32))
        + looked
        + chain_part
    )
    normed = layer_norm(summed, pair_gain).astype(jnp.bfloat16)
    hidden = jax.nn.relu(
        jnp.dot(normed, mlp_in, preferred_element_type=jnp.float32) + mlp_bias
    ).astype(jnp.bfloat16)
    mixed_out = jnp.dot(hidden, mlp_out, preferred_element_type=jnp.float32)
    return (summed + mask_row[:, None] * mixed_out).astype(jnp.bfloat16)


def attention_logits(
    queries, query_points, key_heads, key_points, pair_tile, key_live, bias_weight, point_scale
):
    head_dim = queries.shape[2]
    scores = jnp.einsum(
        "ihd,jhd->ihj", queries, key_heads, preferred_element_type=jnp.float32
    ) * head_dim ** (-0.5)
    biases = jnp.einsum("ijc,ch->ihj", pair_tile, bias_weight, preferred_element_type=jnp.float32)
    query_sq = jnp.sum(query_points * query_points, axis=(1, 3))
    key_sq = jnp.sum(key_points * key_points, axis=(1, 3))
    cross_term = jnp.einsum("iahp,jahp->ihj", query_points, key_points, precision=HIGHEST)
    distance = query_sq[:, :, None] + key_sq.T[None, :, :] - 2.0 * cross_term
    point_weight = math.sqrt(2.0 / (9.0 * query_points.shape[3])) / 2.0
    logits = math.sqrt(1.0 / 3.0) * (
        scores + biases - point_scale[None, :, None] * point_weight * distance
    )
    return jnp.where(key_live[None, None, :], logits, -1e30)


def build_features(row_total, attended, point_sum, pair_sum, frames_rows):
    row_count = row_total.shape[0]
    attended = attended / row_total[:, :, None]
    point_sum = point_sum / row_total[:, None, :, None]
    pair_sum = pair_sum / row_total[:, :, None]
    local_points = to_local(point_sum.reshape(row_count, 3, -1), frames_rows).reshape(
        point_sum.shape
    )
    lengths = jnp.sqrt(jnp.sum(local_points * local_points, axis=1) + 1.0)
    return jnp.concatenate(
        [
            attended.reshape(row_count, -1),
            local_points.reshape(row_count, -1),
            lengths.reshape(row_count, -1),
            pair_sum.reshape(row_count, -1),
        ],
        axis=1,
    ).astype(jnp.bfloat16)


def finish_rows(
    single_rows,
    frames_rows,
    row_total,
    attended,
    point_sum,
    pair_sum,
    head_count,
    head_dim,
    value_count,
    channels,
    w_out,
    single_gain,
    w_frame,
):
    rows_here = single_rows.shape[0]
    features = build_features(
        row_total,
        attended.reshape(rows_here, head_count, head_dim),
        point_sum.reshape(rows_here, 3, head_count, value_count),
        pair_sum.reshape(rows_here, head_count, channels),
        frames_rows,
    )
    update = jnp.dot(features, w_out, preferred_element_type=jnp.float32)
    single_rows = layer_norm(single_rows + update, single_gain)
    frame_step = jnp.dot(
        single_rows.astype(jnp.bfloat16), w_frame, preferred_element_type=jnp.float32
    )
    return (single_rows, update_frames(frames_rows, frame_step))


def shards(
    pair_in,
    single_in,
    frames_in,
    dist_bins,
    res_mask,
    chain_ids,
    w_left,
    w_right,
    dist_embed,
    chain_embed,
    pair_gain,
    mlp_in,
    mlp_bias,
    mlp_out,
    w_qkv,
    w_points,
    bias_weight,
    point_scale,
    w_out,
    single_gain,
    w_frame,
):
    row_count = pair_in.shape[0]
    key_count = pair_in.shape[1]
    channels = pair_in.shape[2]
    head_count = bias_weight.shape[1]
    head_dim = w_qkv.shape[1] // (3 * head_count)
    point_count = w_points.shape[1] // (3 * head_count)
    value_count = point_count - 2 * NQP
    row_start = lax.axis_index("rows") * row_count
    key_start = lax.axis_index("cols") * key_count
    row_live = lax.dynamic_slice_in_dim(res_mask, row_start, row_count).astype(jnp.float32)
    key_mask_int = lax.dynamic_slice_in_dim(res_mask, key_start, key_count)
    key_live = key_mask_int > 0
    pair_mask = row_live[:, None] * key_mask_int.astype(jnp.float32)[None, :]
    same_chain = (
        lax.dynamic_slice_in_dim(chain_ids, row_start, row_count)[:, None]
        == lax.dynamic_slice_in_dim(chain_ids, key_start, key_count)[None, :]
    )
    pair_tile = pair_in
    single = single_in
    frames = frames_in.T
    for cycle_index in range(CYCLES):
        single_bf = single.astype(jnp.bfloat16)
        left_proj = jnp.dot(single_bf, w_left, preferred_element_type=jnp.float32)
        triple = (
            jnp.dot(single_bf, w_qkv, preferred_element_type=jnp.float32)
            .astype(jnp.bfloat16)
            .reshape(row_count, 3, head_count, head_dim)
        )
        own_points = to_global(
            jnp.dot(single_bf, w_points, preferred_element_type=jnp.float32).reshape(
                row_count, 3, head_count * point_count
            ),
            frames,
        ).reshape(row_count, 3, head_count, point_count)
        own_right = jnp.dot(single_bf, w_right, preferred_element_type=jnp.float32).astype(
            jnp.bfloat16
        )
        own_pairs = triple[:, 1:].reshape(row_count, -1)
        own_geometry = own_points[:, :, :, NQP:].reshape(row_count, -1)
        all_right, all_pairs = (
            lax.all_gather(own_right, "rows", axis=0, tiled=True),
            lax.all_gather(own_pairs, "rows", axis=0, tiled=True),
        )
        all_geometry = lax.all_gather(own_geometry, "rows", axis=0, tiled=True)
        right_keys = lax.dynamic_slice_in_dim(all_right, key_start, key_count)
        key_pairs = lax.dynamic_slice_in_dim(all_pairs, key_start, key_count)
        key_geometry = lax.dynamic_slice_in_dim(all_geometry, key_start, key_count)
        key_geometry = key_geometry.reshape(key_count, 3, head_count, point_count - NQP)
        key_heads = key_pairs.reshape(key_count, 2, head_count, head_dim)

        def row_step(inputs):
            return update_row(
                inputs[0],
                inputs[1],
                inputs[2],
                inputs[3],
                inputs[4],
                right_keys,
                dist_embed,
                chain_embed,
                pair_gain,
                mlp_in,
                mlp_bias,
                mlp_out,
            )

        pair_tile = lax.map(
            row_step, (pair_tile, dist_bins[cycle_index], left_proj, pair_mask, same_chain)
        )
        logits = attention_logits(
            triple[:, 0],
            own_points[:, :, :, :NQP],
            key_heads[:, 0],
            key_geometry[:, :, :, :NQP],
            pair_tile,
            key_live,
            bias_weight,
            point_scale,
        )
        row_top = lax.pmax(jnp.max(logits, axis=2), "cols")
        weights = jnp.where(
            key_live[None, None, :], jnp.exp(logits - row_top[:, :, None]), 0.0
        ).astype(jnp.bfloat16)
        row_total = jnp.sum(weights.astype(jnp.float32), axis=2)
        attended = jnp.einsum(
            "ihj,jhd->ihd", weights, key_heads[:, 1], preferred_element_type=jnp.float32
        )
        point_sum = jnp.einsum(
            "ihj,jahp->iahp",
            weights.astype(jnp.float32),
            key_geometry[:, :, :, NQP:],
            precision=HIGHEST,
        )
        pair_sum = jnp.einsum(
            "ihj,ijc->ihc", weights, pair_tile, preferred_element_type=jnp.float32
        )
        row_total, attended, point_sum, pair_sum = (
            lax.psum(row_total.astype(jnp.bfloat16), "cols").astype(jnp.float32),
            lax.psum(attended.reshape(row_count, -1).astype(jnp.bfloat16), "cols").astype(
                jnp.float32
            ),
            lax.psum(point_sum.reshape(row_count, -1).astype(jnp.bfloat16), "cols").astype(
                jnp.float32
            ),
            lax.psum(pair_sum.reshape(row_count, -1).astype(jnp.bfloat16), "cols").astype(
                jnp.float32
            ),
        )
        single, frames = finish_rows(
            single,
            frames,
            row_total,
            attended,
            point_sum,
            pair_sum,
            head_count,
            head_dim,
            value_count,
            channels,
            w_out,
            single_gain,
            w_frame,
        )
    return (pair_tile, single, frames.T)


def solution(mesh):
    in_specs = (
        P(("groups", "rows"), "cols", None),
        P(("groups", "rows"), None),
        P(None, ("groups", "rows")),
        P(None, ("groups", "rows"), "cols"),
        P("groups"),
        P("groups"),
        P(),
        P(),
        P(),
        P(),
        P(),
        P(),
        P(),
        P(),
        P(),
        P(),
        P(),
        P(),
        P(),
        P(),
        P(),
    )
    out_specs = (
        P(("groups", "rows"), "cols", None),
        P(("groups", "rows"), None),
        P(None, ("groups", "rows")),
    )
    return jax.shard_map(shards, mesh=mesh, in_specs=in_specs, out_specs=out_specs, check_vma=False)
```

profile of v0, /device:TPU:0, one launch (start us, length us, event | category | flops | bytes accessed | tf_op | source)
XLA Modules:
  0.0 194.5 jit_solution(276466925991388244)
XLA Ops:
  0.6 0.8 convert_element_type.191
  1.4 0.7 dynamic-slice_convert_fusion
  2.2 0.7 convert_element_type.192
  2.9 1.0 fusion.123
  4.0 1.0 convolution_convert_fusion.9
  5.0 23.2 %all_gather.18 = bf16[128,128]{1,0:T(8,128)(2,1)S(1)} all-gather(bf16[8,128]{1,0:T(8,128)(2,1)S(1)} %convolution_convert_fusion.9), channel_id=1, replica_groups=mesh['groups'=2,'rows'=16,'cols'=1] {'rows'}, dimensions={0}, use_global_device_ids=true | all-gather | bytes 34816 | tf_op jit(solution)/shard_map/all_gather | solution.py:222
  28.3 1.3 slice_bitcast_fusion.8
  29.6 0.7 dynamic_slice.49
  30.3 0.7 broadcast_compare_fusion
  31.1 33.2 %while.20 = (s32[]{:T(128)}, bf16[8,128,128]{1,2,0:T(8,128)(2,1)S(1)}, bf16[8,128,128]{2,1,0:T(8,128)(2,1)}, f32[8,128]{1,0:T(8,128)S(1)}, f32[8,128]{1,0:T(8,12...) while((s32[]{:T(128)}, ...), condition=%wide.region_3.4_spmd, body=%wide.region_0.3_spmd.sunk | while | flops 34556160 | bytes 772905 | solution.py:248
  31.1 0.7 bitcast_convert_fusion.6
  31.9 0.8 constant_dynamic-slice_fusion.8
  32.8 1.0 fusion.202
  33.8 1.5 fusion.203
  35.3 0.7 bitcast_convert_fusion.6
  36.0 0.8 constant_dynamic-slice_fusion.8
  36.9 1.0 fusion.202
  37.9 1.5 fusion.203
  39.4 0.7 bitcast_convert_fusion.6
  40.2 0.8 constant_dynamic-slice_fusion.8
  41.1 1.0 fusion.202
  42.1 1.5 fusion.203
  43.6 0.7 bitcast_convert_fusion.6
  44.4 0.8 constant_dynamic-slice_fusion.8
  45.2 1.0 fusion.202
  46.2 1.5 fusion.203
  47.7 0.7 bitcast_convert_fusion.6
  48.5 0.8 constant_dynamic-slice_fusion.8
  49.4 1.0 fusion.202
  50.4 1.5 fusion.203
  51.9 0.7 bitcast_convert_fusion.6
  52.7 0.8 constant_dynamic-slice_fusion.8
  53.5 1.0 fusion.202
  54.6 1.5 fusion.203
  56.0 0.7 bitcast_convert_fusion.6
  56.8 0.8 constant_dynamic-slice_fusion.8
  57.7 1.0 fusion.202
  58.7 1.5 fusion.203
  60.2 0.7 bitcast_convert_fusion.6
  61.0 0.8 constant_dynamic-slice_fusion.8
  61.9 1.0 fusion.202
  62.9 1.5 fusion.203
  65.9 18.1 %all_gather.20 = f32[128,432]{1,0:T(8,128)S(1)} all-gather(f32[8,432]{1,0:T(8,128)S(1)} %reshape.270), channel_id=1, replica_groups=mesh['groups'=2,'rows'=16,'cols'=1] {'rows'}, dimensions={0}, use_global_device_ids=true | all-gather | bytes 235008 | tf_op jit(solution)/shard_map/all_gather | solution.py:225
  85.2 19.0 %all_gather.19 = bf16[128,384]{1,0:T(8,128)(2,1)S(1)} all-gather(bf16[8,384]{1,0:T(8,128)(2,1)S(1)} %reshape.265), channel_id=1, replica_groups=mesh['groups'=2,'rows'=16,'cols'=1] {'rows'}, dimensions={0}, use_global_device_ids=true | all-gather | bytes 104448 | tf_op jit(solution)/shard_map/all_gather | solution.py:223
  105.8 0.7 copy.80
  107.1 0.7 broadcast_subtract_fusion.1
  107.9 0.9 multiply_reduce_fusion.7
  108.9 0.8 copy.83
  109.6 1.0 fusion.92
  110.6 0.8 concatenate.11
  111.4 1.1 fusion.118
  113.1 17.6 %all_gather.21 = bf16[128,128]{1,0:T(8,128)(2,1)S(1)} all-gather(bf16[8,128]{1,0:T(8,128)(2,1)S(1)} %convolution_convert_fusion.8), channel_id=1, replica_groups=mesh['groups'=2,'rows'=16,'cols'=1] {'rows'}, dimensions={0}, use_global_device_ids=true | all-gather | bytes 34816 | tf_op jit(solution)/shard_map/all_gather | solution.py:222
  130.9 17.7 %while.21 = (s32[]{:T(128)}, bf16[8,128,128]{1,2,0:T(8,128)(2,1)S(1)}, bf16[8,128,128]{1,2,0:T(8,128)(2,1)S(1)}, f32[8,128]{1,0:T(8,128)}, f32[8,128]{1,0:T(8,12...) while((s32[]{:T(128)}, ...), condition=%wide.region_14.15_spmd, body=%wide.region_11.14_spmd.sunk | while | flops 34556160 | bytes 641833 | solution.py:248
  131.0 0.7 fusion.207
  133.2 0.7 fusion.207
  135.4 0.7 fusion.207
  137.6 0.7 fusion.207
  139.8 0.7 fusion.207
  142.1 0.7 fusion.207
  144.3 0.7 fusion.207
  146.5 0.7 fusion.207
  148.7 0.9 copy.108
  151.5 19.4 %all_gather.23 = f32[128,432]{1,0:T(8,128)S(1)} all-gather(f32[8,432]{1,0:T(8,128)S(1)} %reshape.281), channel_id=1, replica_groups=mesh['groups'=2,'rows'=16,'cols'=1] {'rows'}, dimensions={0}, use_global_device_ids=true | all-gather | bytes 235008 | tf_op jit(solution)/shard_map/all_gather | solution.py:225
  172.0 17.8 %all_gather.22 = bf16[128,384]{1,0:T(8,128)(2,1)S(1)} all-gather(bf16[8,384]{1,0:T(8,128)(2,1)S(1)} %reshape.276), channel_id=1, replica_groups=mesh['groups'=2,'rows'=16,'cols'=1] {'rows'}, dimensions={0}, use_global_device_ids=true | all-gather | bytes 104448 | tf_op jit(solution)/shard_map/all_gather | solution.py:223
  (299 shorter events, 26.5 us)
Async XLA Ops:
  0.6 110.8 %copy-start = (bf16[2112,384]{1,0:T(8,128)(2,1)S(1)}, bf16[2112,384]{1,0:T(8,128)(2,1)}, u32[]{:S(2)}) copy-start(bf16[2112,384]{1,0:T(8,128)(2,1)} %param.43) | copy-start | bytes 4866052
  31.1 33.3 %copy-start.25 = (s32[128]{0:T(128)S(1)}, s32[128]{0:T(128)}, u32[]{:S(2)}) copy-start(s32[128]{0:T(128)} %param.29) | copy-start | bytes 1540
  31.1 33.3 %copy-start.3 = (bf16[384,576]{0,1:T(8,128)(2,1)S(1)}, bf16[384,576]{0,1:T(8,128)(2,1)}, u32[]{:S(2)}) copy-start(bf16[384,576]{0,1:T(8,128)(2,1)} %param.40) | copy-start | bytes 1327108
  31.1 33.6 %copy-start.19 = (f32[12,8]{0,1:T(8,128)S(1)}, f32[12,8]{0,1:T(8,128)}, u32[]{:S(2)}) copy-start(f32[12,8]{0,1:T(8,128)} %param.27) | copy-start | bytes 1156
  64.3 0.9 copy-start.12
  64.4 0.9 copy-start.22
  64.4 40.2 %copy-start.27 = (pred[128]{0:T(512)(128)(4,1)}, pred[128]{0:T(512)(128)(4,1)S(1)}, u32[]{:S(2)}) copy-start(pred[128]{0:T(512)(128)(4,1)S(1)} %broadcast_compare_fusion.1) | copy-start | bytes 388
  64.6 19.7 %copy-start.26 = (f32[12]{0:T(128)S(1)}, f32[12]{0:T(128)}, u32[]{:S(2)}) copy-start(f32[12]{0:T(128)} %param.42) | copy-start | bytes 148
  64.9 42.0 %copy-start.15 = (f32[8,3]{0,1:T(4,128)}, f32[8,3]{0,1:T(4,128)S(1)}, u32[]{:S(2)}) copy-start(f32[8,3]{0,1:T(4,128)S(1)} %slice.143) | copy-start | bytes 292
  65.3 19.5 %copy-start.4 = (bf16[384,576]{0,1:T(8,128)(2,1)S(1)}, bf16[384,576]{0,1:T(8,128)(2,1)}, u32[]{:S(2)}) copy-start(bf16[384,576]{0,1:T(8,128)(2,1)} %param.39) | copy-start | bytes 1327108
  65.8 38.6 %copy-start.17 = (bf16[128,12]{0,1:T(8,128)(2,1)S(1)}, bf16[128,12]{0,1:T(8,128)(2,1)}, u32[]{:S(2)}) copy-start(bf16[128,12]{0,1:T(8,128)(2,1)} %param.41) | copy-start | bytes 9220
  84.4 0.9 copy-start.20
  104.9 1.8 copy-start.29
  104.9 2.0 %copy-start.16 = (bf16[8,12]{0,1:T(8,128)(2,1)}, bf16[8,12]{0,1:T(8,128)(2,1)S(1)}, u32[]{:S(2)}) copy-start(bf16[8,12]{0,1:T(8,128)(2,1)S(1)} %get-tuple-element.307) | copy-start | bytes 580
  106.7 6.1 %copy-start.13 = (f32[384]{0:T(512)S(1)}, f32[384]{0:T(512)}, u32[]{:S(2)}) copy-start(f32[384]{0:T(512)} %param.44) | copy-start | bytes 4612
  106.7 6.1 %copy-start.5 = (bf16[384,128]{1,0:T(8,128)(2,1)S(1)}, bf16[384,128]{1,0:T(8,128)(2,1)}, u32[]{:S(2)}) copy-start(bf16[384,128]{1,0:T(8,128)(2,1)} %param.31) | copy-start | bytes 294916
  106.7 6.3 %copy-start.6 = (bf16[384,128]{1,0:T(8,128)(2,1)S(1)}, bf16[384,128]{1,0:T(8,128)(2,1)}, u32[]{:S(2)}) copy-start(bf16[384,128]{1,0:T(8,128)(2,1)} %param.32) | copy-start | bytes 294916
  106.9 23.9 %copy-start.1 = (bf16[128,512]{1,0:T(8,128)(2,1)S(1)}, bf16[128,512]{1,0:T(8,128)(2,1)}, u32[]{:S(2)}) copy-start(bf16[128,512]{1,0:T(8,128)(2,1)} %get-tuple-element.600) | copy-start | bytes 393220
  106.9 23.9 %copy-start.2 = (bf16[512,128]{1,0:T(8,128)(2,1)S(1)}, bf16[512,128]{1,0:T(8,128)(2,1)}, u32[]{:S(2)}) copy-start(bf16[512,128]{1,0:T(8,128)(2,1)} %get-tuple-element.601) | copy-start | bytes 393220
  106.9 23.9 %copy-start.7 = (f32[512]{0:T(512)S(1)}, f32[512]{0:T(512)}, u32[]{:S(2)}) copy-start(f32[512]{0:T(512)} %get-tuple-element.602) | copy-start | bytes 6148
  107.0 23.9 %copy-start.8 = (bf16[2,128]{1,0:T(2,128)(2,1)S(1)}, bf16[2,128]{1,0:T(2,128)(2,1)}, u32[]{:S(2)}) copy-start(bf16[2,128]{1,0:T(2,128)(2,1)} %get-tuple-element.603) | copy-start | bytes 1540
  107.0 23.9 %copy-start.9 = (f32[128]{0:T(128)S(1)}, f32[128]{0:T(128)}, u32[]{:S(2)}) copy-start(f32[128]{0:T(128)} %get-tuple-element.604) | copy-start | bytes 1540
  107.1 23.8 %copy-start.23 = (pred[8,128]{1,0:T(8,128)(4,1)S(1)}, pred[8,128]{1,0:T(8,128)(4,1)}, u32[]{:S(2)}) copy-start(pred[8,128]{1,0:T(8,128)(4,1)} %copy-done.22) | copy-start | bytes 3076
  107.1 23.8 %copy-start.24 = (bf16[15,128]{1,0:T(8,128)(2,1)S(1)}, bf16[15,128]{1,0:T(8,128)(2,1)}, u32[]{:S(2)}) copy-start(bf16[15,128]{1,0:T(8,128)(2,1)} %get-tuple-element.607) | copy-start | bytes 11524
  130.9 18.6 %copy-start.11 = (bf16[384,6]{0,1:T(8,128)(2,1)S(1)}, bf16[384,6]{0,1:T(8,128)(2,1)}, u32[]{:S(2)}) copy-start(bf16[384,6]{0,1:T(8,128)(2,1)} %param.45) | copy-start | bytes 13828
  150.3 20.9 %copy-start.21 = (f32[12]{0:T(128)S(1)}, f32[12]{0:T(128)}, u32[]{:S(2)}) copy-start(f32[12]{0:T(128)} %copy-done.20) | copy-start | bytes 148
  151.3 38.7 %copy-start.18 = (bf16[128,12]{0,1:T(8,128)(2,1)S(1)}, bf16[128,12]{0,1:T(8,128)(2,1)}, u32[]{:S(2)}) copy-start(bf16[128,12]{0,1:T(8,128)(2,1)} %param.41) | copy-start | bytes 9220
  151.4 38.7 %copy-start.28 = (pred[128]{0:T(512)(128)(4,1)S(1)}, pred[128]{0:T(512)(128)(4,1)}, u32[]{:S(2)}) copy-start(pred[128]{0:T(512)(128)(4,1)} %copy-done.27) | copy-start | bytes 388
  172.0 20.1 %copy-start.14 = (f32[384]{0:T(512)S(1)}, f32[384]{0:T(512)}, u32[]{:S(2)}) copy-start(f32[384]{0:T(512)} %param.44) | copy-start | bytes 4612
  192.8 1.7 copy-start.10
where the time goes:
time: 197 us; the launch traced here: 195 us
  blocking collectives  115 us (58%)
  matrix products  35.8 us (18%)
  local copies, waits for them, and re-layouts  30 us (15%)
  other arithmetic  11.5 us (6%)
    all_gather x2, blocking collectives, shards(): lax.all_gather(own_right, 'rows', axis=0, tiled=True)  40.7 us
    all_gather x2, blocking collectives, shards(): all_geometry = lax.all_gather(own_geometry, 'rows', axis=0, tiled=True)  37.6 us
    all_gather x2, blocking collectives, shards(): lax.all_gather(own_pairs, 'rows', axis=0, tiled=True)  36.8 us
    dot_general x16, matrix products, update_row(): mixed_out = jnp.dot(hidden, mlp_out, preferred_element_type=jnp.float32)  15.4 us
    dot_general x16, matrix products, update_row(): looked = jnp.dot(onehot, dist_embed, preferred_element_type=jnp.float32)  9.72 us
    dynamic_slice x16, local copies, waits for them, and re-layouts, shards(): lax.map(row_step, (pair_tile, dist_bins[cycle_index], left_proj, pair_mas...  7.02 us
    convert_element_type x16, other arithmetic, update_row(): chain_embed[1].astype(jnp.float32)  5.94 us
    eq x16, local copies, waits for them, and re-layouts, update_row(): bins_row[:, None]  5.66 us

commit v1 on v0

--- a/solution.py
+++ b/solution.py
@@ -222,7 +222,23 @@
             lax.all_gather(own_right, "rows", axis=0, tiled=True),
             lax.all_gather(own_pairs, "rows", axis=0, tiled=True),
         )
-        all_geometry = lax.all_gather(own_geometry, "rows", axis=0, tiled=True)
+        blocks_here = []
+        sides = jax.lax.psum(1, "rows")
+        for s in range(sides):
+            blocks_here.append((s, (s + 1) % sides))
+        pieces_in = []
+        for s in range(sides):
+            pieces_in.append((s, (s - 1) % sides))
+        inter, built = ([own_geometry], [own_geometry])
+        for _ in range(sides // 2):
+            inter.append(jax.lax.ppermute(inter[-1], "rows", blocks_here))
+        for _ in range((sides - 1) // 2):
+            built.append(jax.lax.ppermute(built[-1], "rows", pieces_in))
+        all_geometry = jnp.roll(
+            jnp.concatenate([*inter[::-1], *built[1:]], axis=0),
+            (jax.lax.axis_index("rows") - sides // 2) * own_geometry.shape[0],
+            axis=0,
+        )
         right_keys = lax.dynamic_slice_in_dim(all_right, key_start, key_count)
         key_pairs = lax.dynamic_slice_in_dim(all_pairs, key_start, key_count)
         key_geometry = lax.dynamic_slice_in_dim(all_geometry, key_start, key_count)

time: 197 us -> 218 us (1.11)
  starting transfers between devices: 0 us -> 54.2 us
  blocking collectives: 115 us -> 73.9 us
  waiting for transfers between devices: 0 us -> 17.3 us
  matrix products: 35.8 us -> 27.6 us
  other arithmetic: 11.5 us -> 5.43 us
  local copies, waits for them, and re-layouts: 30 us -> 34.8 us
    ppermute x0 -> x30, starting transfers between devices: none -> 54.2 us  [the longest x14 52.4 us: shards(): built.append(jax.lax.ppermute(built[-1], 'rows', pieces_in))]
    all_gather x2 -> x0, blocking collectives: 37.6 us -> none  [shards(): all_geometry = lax.all_gather(own_geometry, 'rows', axis=0, tiled=True)]
    ppermute x0 -> x30, waiting for transfers between devices: none -> 17.3 us  [the longest x16 10.5 us: shards(): inter.append(jax.lax.ppermute(inter[-1], 'rows', blocks_here))]
    dot_general x16, matrix products: 15.4 us -> 7.39 us  [update_row(): mixed_out = jnp.dot(hidden, mlp_out, preferred_element_type=jnp.float32)]
    convert_element_type x16, other arithmetic: 5.94 us -> 0.08 us  [update_row(): chain_embed[1].astype(jnp.float32)]
    broadcast_in_dim x16, local copies, waits for them, and re-layouts: 0.16 us -> 5.44 us  [update_row(): jnp.where(same_row[:, None], chain_embed[1].astype(jnp.float32), chain_em...]
    all_gather x2, blocking collectives: 40.7 us -> 37.4 us  [shards(): lax.all_gather(own_right, 'rows', axis=0, tiled=True)]
  transfers between devices with their start and end apart: 0 -> 30, of which waited for: 0 -> 14; matrix products, arithmetic and copies ran while one was open for 0% -> 23% of each run, Pallas kernels for 0% -> 0%
where the time goes in v1:
time: 218 us; the launch traced here: 216 us
  blocking collectives  73.9 us (34%)
  starting transfers between devices  54.2 us (25%)
  local copies, waits for them, and re-layouts  34.8 us (16%)
  matrix products  27.6 us (13%)
  waiting for transfers between devices  17.3 us (8%)
  other arithmetic  5.43 us (2%)
    ppermute x14, starting transfers between devices, shards(): built.append(jax.lax.ppermute(built[-1], 'rows', pieces_in))  52.4 us
    all_gather x2, blocking collectives, shards(): lax.all_gather(own_right, 'rows', axis=0, tiled=True)  37.4 us
    all_gather x2, blocking collectives, shards(): lax.all_gather(own_pairs, 'rows', axis=0, tiled=True)  36.5 us
    ppermute x16, waiting for transfers between devices, shards(): inter.append(jax.lax.ppermute(inter[-1], 'rows', blocks_here))  10.5 us
    dot_general x16, matrix products, update_row(): looked = jnp.dot(onehot, dist_embed, preferred_element_type=jnp.float32)  9.63 us
    dot_general x16, matrix products, update_row(): mixed_out = jnp.dot(hidden, mlp_out, preferred_element_type=jnp.float32)  7.39 us
    dynamic_slice x16, local copies, waits for them, and re-layouts, shards(): lax.map(row_step, (pair_tile, dist_bins[cycle_index], left_proj, pair_mas...  7.06 us
    ppermute x14, waiting for transfers between devices, shards(): built.append(jax.lax.ppermute(built[-1], 'rows', pieces_in))  6.78 us
  transfers between devices with their start and end apart: 30, of which 14 were waited for; matrix products, arithmetic and copies ran while one was open for 23% of the time, Pallas kernels for 0%

profile of v1, /device:TPU:0, one launch (start us, length us, event | category | flops | bytes accessed | tf_op | source)
XLA Modules:
  0.0 215.7 jit_solution(17448987245354460827)
XLA Ops:
  0.8 0.9 copy.68
  1.8 0.7 convert_element_type.192
  2.5 1.2 fusion.126
  5.1 5.0 %collective-permute-start.8 = (f32[8,432]{1,0:T(8,128)S(1)}, f32[8,432]{1,0:T(8,128)S(1)}, u32[]{:S(2)}, u32[]{:S(2)}) collective-permute-start(f32[8,432]{1,0:T(8,128)S(1)} %reshape.270), channel_id=1, source_target_pairs={{0,15},{1,0},{2,1},{3,2},{4,3},{5,4},{6,5},{7,6},{8,7},{9,8},{10,9... | collective-permute-start | bytes 41480 | tf_op jit(solution)/shard_map/ppermute | solution.py:236
  11.3 19.4 %all_gather.12 = bf16[128,128]{1,0:T(8,128)(2,1)S(1)} all-gather(bf16[8,128]{1,0:T(8,128)(2,1)S(1)} %convolution_convert_fusion.9), channel_id=1, replica_groups=mesh['groups'=2,'rows'=16,'cols'=1] {'rows'}, dimensions={0}, use_global_device_ids=true | all-gather | bytes 34816 | tf_op jit(solution)/shard_map/all_gather | solution.py:222
  31.3 14.0 %while.20 = (s32[]{:T(128)}, bf16[8,128,128]{1,2,0:T(8,128)(2,1)S(1)}, bf16[8,128,128]{2,1,0:T(8,128)(2,1)}, f32[8,128]{1,0:T(8,128)S(1)}, f32[8,128]{1,0:T(8,12...) while((s32[]{:T(128)}, ...), condition=%wide.region_3.4_spmd, body=%wide.region_0.3_spmd.sunk | while | flops 34556160 | bytes 772897 | solution.py:264
  31.3 0.8 constant_dynamic-slice_fusion.8
  33.1 0.8 constant_dynamic-slice_fusion.8
  34.9 0.8 constant_dynamic-slice_fusion.8
  36.6 0.8 constant_dynamic-slice_fusion.8
  38.4 0.8 constant_dynamic-slice_fusion.8
  40.1 0.8 constant_dynamic-slice_fusion.8
  41.8 0.8 constant_dynamic-slice_fusion.8
  43.6 0.8 constant_dynamic-slice_fusion.8
  45.6 4.5 %collective-permute-start.9 = (f32[8,432]{1,0:T(8,128)S(1)}, f32[8,432]{1,0:T(8,128)S(1)}, u32[]{:S(2)}, u32[]{:S(2)}) collective-permute-start(f32[8,432]{1,0:T(8,128)S(1)} %collective-permute-done.8), channel_id=1, source_target_pairs={{0,15},{1,0},{2,1},{3,2},{4,3},{5,4},{6,5},{7,6},{8,7},{9,8},{10,9... | collective-permute-start | bytes 41480 | tf_op jit(solution)/shard_map/ppermute | solution.py:236
  50.1 1.2 collective-permute-done.2
  51.3 0.8 fusion.114
  52.0 4.4 %collective-permute-start.10 = (f32[8,432]{1,0:T(8,128)S(1)}, f32[8,432]{1,0:T(8,128)S(1)}, u32[]{:S(2)}, u32[]{:S(2)}) collective-permute-start(f32[8,432]{1,0:T(8,128)S(1)} %collective-permute-done.9), channel_id=1, source_target_pairs={{0,15},{1,0},{2,1},{3,2},{4,3},{5,4},{6,5},{7,6},{8,7},{9,8},{10,9... | collective-permute-start | bytes 41480 | tf_op jit(solution)/shard_map/ppermute | solution.py:236
  57.9 4.4 %collective-permute-start.11 = (f32[8,432]{1,0:T(8,128)S(1)}, f32[8,432]{1,0:T(8,128)S(1)}, u32[]{:S(2)}, u32[]{:S(2)}) collective-permute-start(f32[8,432]{1,0:T(8,128)S(1)} %collective-permute-done.10), channel_id=1, source_target_pairs={{0,15},{1,0},{2,1},{3,2},{4,3},{5,4},{6,5},{7,6},{8,7},{9,8},{10,9... | collective-permute-start | bytes 41480 | tf_op jit(solution)/shard_map/ppermute | solution.py:236
  63.8 4.5 %collective-permute-start.12 = (f32[8,432]{1,0:T(8,128)S(1)}, f32[8,432]{1,0:T(8,128)S(1)}, u32[]{:S(2)}, u32[]{:S(2)}) collective-permute-start(f32[8,432]{1,0:T(8,128)S(1)} %collective-permute-done.11), channel_id=1, source_target_pairs={{0,15},{1,0},{2,1},{3,2},{4,3},{5,4},{6,5},{7,6},{8,7},{9,8},{10,9... | collective-permute-start | bytes 41480 | tf_op jit(solution)/shard_map/ppermute | solution.py:236
  69.7 4.4 %collective-permute-start.13 = (f32[8,432]{1,0:T(8,128)S(1)}, f32[8,432]{1,0:T(8,128)S(1)}, u32[]{:S(2)}, u32[]{:S(2)}) collective-permute-start(f32[8,432]{1,0:T(8,128)S(1)} %collective-permute-done.12), channel_id=1, source_target_pairs={{0,15},{1,0},{2,1},{3,2},{4,3},{5,4},{6,5},{7,6},{8,7},{9,8},{10,9... | collective-permute-start | bytes 41480 | tf_op jit(solution)/shard_map/ppermute | solution.py:236
  74.7 18.2 %all_gather.13 = bf16[128,384]{1,0:T(8,128)(2,1)S(1)} all-gather(bf16[8,384]{1,0:T(8,128)(2,1)S(1)} %reshape.265), channel_id=1, replica_groups=mesh['groups'=2,'rows'=16,'cols'=1] {'rows'}, dimensions={0}, use_global_device_ids=true | all-gather | bytes 104448 | tf_op jit(solution)/shard_map/all_gather | solution.py:223
  93.6 0.7 copy.80
  94.4 1.2 collective-permute-start.14
  95.8 1.3 collective-permute-done.14
  97.8 1.1 fusion.119
  99.0 0.9 fusion.51
  100.4 1.1 copy.78
  103.2 0.8 fusion.109
  104.0 0.8 fusion.128
  107.0 0.8 collective-permute-start.15
  107.7 3.8 %collective-permute-start.23 = (f32[8,432]{1,0:T(8,128)S(1)}, f32[8,432]{1,0:T(8,128)S(1)}, u32[]{:S(2)}, u32[]{:S(2)}) collective-permute-start(f32[8,432]{1,0:T(8,128)S(1)} %reshape.281), channel_id=1, source_target_pairs={{0,15},{1,0},{2,1},{3,2},{4,3},{5,4},{6,5},{7,6},{8,7},{9,8},{10,9... | collective-permute-start | bytes 41480 | tf_op jit(solution)/shard_map/ppermute | solution.py:236
  111.6 1.2 collective-permute-done.15
  113.0 5.7 %collective-permute-done.16 = f32[8,432]{1,0:T(8,128)S(1)} collective-permute-done((f32[8,432]{1,0:T(8,128)S(1)}, f32[8,432]{1,0:T(8,128)S(1)}, u32[]{:S(2)}, u32[]{:S(2)}) %collective-permute-start.16) | collective-permute-done | bytes 13856 | tf_op jit(solution)/shard_map/ppermute | solution.py:234
  118.7 18.1 %all_gather.14 = bf16[128,128]{1,0:T(8,128)(2,1)S(1)} all-gather(bf16[8,128]{1,0:T(8,128)(2,1)S(1)} %convolution_convert_fusion.8), channel_id=1, replica_groups=mesh['groups'=2,'rows'=16,'cols'=1] {'rows'}, dimensions={0}, use_global_device_ids=true | all-gather | bytes 34816 | tf_op jit(solution)/shard_map/all_gather | solution.py:222
  136.9 1.2 collective-permute-start.24
  138.2 28.3 %while.21 = (s32[]{:T(128)}, bf16[8,128,128]{1,2,0:T(8,128)(2,1)S(1)}, bf16[8,128,128]{1,2,0:T(8,128)(2,1)S(1)}, f32[8,128]{1,0:T(8,128)}, f32[8,128]{1,0:T(8,12...) while((s32[]{:T(128)}, ...), condition=%wide.region_14.16_spmd, body=%wide.region_11.15_spmd.sunk | while | flops 34556160 | bytes 641825 | solution.py:264
  138.3 0.7 fusion.210
  140.3 0.9 fusion.211
  141.8 0.7 fusion.210
  143.9 0.9 fusion.211
  145.3 0.7 fusion.210
  147.4 0.9 fusion.211
  148.9 0.7 fusion.210
  150.9 0.9 fusion.211
  152.4 0.7 fusion.210
  154.5 0.9 fusion.211
  155.9 0.7 fusion.210
  158.0 0.9 fusion.211
  159.5 0.7 fusion.210
  161.5 0.9 fusion.211
  163.0 0.7 fusion.210
  165.1 0.9 fusion.211
  166.6 4.5 %collective-permute-start.25 = (f32[8,432]{1,0:T(8,128)S(1)}, f32[8,432]{1,0:T(8,128)S(1)}, u32[]{:S(2)}, u32[]{:S(2)}) collective-permute-start(f32[8,432]{1,0:T(8,128)S(1)} %collective-permute-done.24), channel_id=1, source_target_pairs={{0,15},{1,0},{2,1},{3,2},{4,3},{5,4},{6,5},{7,6},{8,7},{9,8},{10,9... | collective-permute-start | bytes 41480 | tf_op jit(solution)/shard_map/ppermute | solution.py:236
  171.3 1.2 collective-permute-done.25
  172.5 4.4 %collective-permute-start.26 = (f32[8,432]{1,0:T(8,128)S(1)}, f32[8,432]{1,0:T(8,128)S(1)}, u32[]{:S(2)}, u32[]{:S(2)}) collective-permute-start(f32[8,432]{1,0:T(8,128)S(1)} %collective-permute-done.25), channel_id=1, source_target_pairs={{0,15},{1,0},{2,1},{3,2},{4,3},{5,4},{6,5},{7,6},{8,7},{9,8},{10,9... | collective-permute-start | bytes 41480 | tf_op jit(solution)/shard_map/ppermute | solution.py:236
  177.4 1.0 collective-permute-done.26
  178.4 4.4 %collective-permute-start.27 = (f32[8,432]{1,0:T(8,128)S(1)}, f32[8,432]{1,0:T(8,128)S(1)}, u32[]{:S(2)}, u32[]{:S(2)}) collective-permute-start(f32[8,432]{1,0:T(8,128)S(1)} %collective-permute-done.26), channel_id=1, source_target_pairs={{0,15},{1,0},{2,1},{3,2},{4,3},{5,4},{6,5},{7,6},{8,7},{9,8},{10,9... | collective-permute-start | bytes 41480 | tf_op jit(solution)/shard_map/ppermute | solution.py:236
  183.1 1.1 collective-permute-done.27
  184.2 4.4 %collective-permute-start.28 = (f32[8,432]{1,0:T(8,128)S(1)}, f32[8,432]{1,0:T(8,128)S(1)}, u32[]{:S(2)}, u32[]{:S(2)}) collective-permute-start(f32[8,432]{1,0:T(8,128)S(1)} %collective-permute-done.27), channel_id=1, source_target_pairs={{0,15},{1,0},{2,1},{3,2},{4,3},{5,4},{6,5},{7,6},{8,7},{9,8},{10,9... | collective-permute-start | bytes 41480 | tf_op jit(solution)/shard_map/ppermute | solution.py:236
  188.7 18.2 %all_gather.15 = bf16[128,384]{1,0:T(8,128)(2,1)S(1)} all-gather(bf16[8,384]{1,0:T(8,128)(2,1)S(1)} %reshape.276), channel_id=1, replica_groups=mesh['groups'=2,'rows'=16,'cols'=1] {'rows'}, dimensions={0}, use_global_device_ids=true | all-gather | bytes 104448 | tf_op jit(solution)/shard_map/all_gather | solution.py:223
  206.9 0.8 copy.108
  207.9 1.2 collective-permute-start.29
  209.3 1.3 collective-permute-done.29
  (421 shorter events, 43.0 us)
Async XLA Ops:
  0.6 101.5 %copy-start = (bf16[2112,384]{1,0:T(8,128)(2,1)S(1)}, bf16[2112,384]{1,0:T(8,128)(2,1)}, u32[]{:S(2)}) copy-start(bf16[2112,384]{1,0:T(8,128)(2,1)} %param.45) | copy-start | bytes 4866052
  0.6 9.4 %copy-start.42 = (s32[128]{0:T(128)S(1)}, s32[128]{0:T(128)}, u32[]{:S(2)}) copy-start(s32[128]{0:T(128)} %param.31) | copy-start | bytes 1540
  0.7 9.5 %copy-start.40 = (s32[128]{0:T(128)S(1)}, s32[128]{0:T(128)}, u32[]{:S(2)}) copy-start(s32[128]{0:T(128)} %param.32) | copy-start | bytes 1540
  0.7 9.6 %copy-start.6 = (bf16[384,128]{1,0:T(8,128)(2,1)S(1)}, bf16[384,128]{1,0:T(8,128)(2,1)}, u32[]{:S(2)}) copy-start(bf16[384,128]{1,0:T(8,128)(2,1)} %param.34) | copy-start | bytes 294916
  0.7 9.8 %copy-start.5 = (bf16[384,128]{1,0:T(8,128)(2,1)S(1)}, bf16[384,128]{1,0:T(8,128)(2,1)}, u32[]{:S(2)}) copy-start(bf16[384,128]{1,0:T(8,128)(2,1)} %param.33) | copy-start | bytes 294916
  0.7 9.9 %copy-start.32 = (s32[2,8,128]{2,1,0:T(8,128)S(1)}, s32[2,8,128]{2,1,0:T(8,128)}, u32[]{:S(2)}) copy-start(s32[2,8,128]{2,1,0:T(8,128)} %param.30) | copy-start | bytes 24580
  0.7 30.5 %copy-start.41 = (bf16[15,128]{1,0:T(8,128)(2,1)S(1)}, bf16[15,128]{1,0:T(8,128)(2,1)}, u32[]{:S(2)}) copy-start(bf16[15,128]{1,0:T(8,128)(2,1)} %param.35) | copy-start | bytes 11524
  0.7 30.5 %copy-start.9 = (bf16[2,128]{1,0:T(2,128)(2,1)S(1)}, bf16[2,128]{1,0:T(2,128)(2,1)}, u32[]{:S(2)}) copy-start(bf16[2,128]{1,0:T(2,128)(2,1)} %param.36) | copy-start | bytes 1540
  0.7 30.5 %copy-start.15 = (f32[128]{0:T(128)S(1)}, f32[128]{0:T(128)}, u32[]{:S(2)}) copy-start(f32[128]{0:T(128)} %param.37) | copy-start | bytes 1540
  0.7 30.5 %copy-start.1 = (bf16[128,512]{1,0:T(8,128)(2,1)S(1)}, bf16[128,512]{1,0:T(8,128)(2,1)}, u32[]{:S(2)}) copy-start(bf16[128,512]{1,0:T(8,128)(2,1)} %param.38) | copy-start | bytes 393220
  0.7 30.5 %copy-start.8 = (f32[512]{0:T(512)S(1)}, f32[512]{0:T(512)}, u32[]{:S(2)}) copy-start(f32[512]{0:T(512)} %param.39) | copy-start | bytes 6148
  0.8 30.5 %copy-start.2 = (bf16[512,128]{1,0:T(8,128)(2,1)S(1)}, bf16[512,128]{1,0:T(8,128)(2,1)}, u32[]{:S(2)}) copy-start(bf16[512,128]{1,0:T(8,128)(2,1)} %param.40) | copy-start | bytes 393220
  1.7 91.9 %copy-start.12 = (f32[8,3,3]{0,2,1:T(4,128)}, f32[8,3,3]{0,2,1:T(4,128)S(1)}, u32[]{:S(2)}) copy-start(f32[8,3,3]{0,2,1:T(4,128)S(1)} %reshape.268) | copy-start | bytes 868
  1.8 29.4 %copy-start.10 = (f32[8,3,3]{2,1,0:T(4,128)}, f32[8,3,3]{2,1,0:T(4,128)S(1)}, u32[]{:S(2)}) copy-start(f32[8,3,3]{2,1,0:T(4,128)S(1)} %copy.69) | copy-start | bytes 868
  4.5 26.2 %collective-permute-start = (f32[8,432]{1,0:T(8,128)S(1)}, f32[8,432]{1,0:T(8,128)S(1)}, u32[]{:S(2)}, u32[]{:S(2)}) collective-permute-start(f32[8,432]{1,0:T(8,128)S(1)} %reshape.270), channel_id=1, source_target_pairs={{0,1},{1,2},{2,3},{3,4},{4,5},{5,6},{6,7},{7,8},{8,9},{9,10},{10,1... | collective-permute-start | bytes 41480 | tf_op jit(solution)/shard_map/ppermute | solution.py:234
  5.1 40.6 %collective-permute-start.8 = (f32[8,432]{1,0:T(8,128)S(1)}, f32[8,432]{1,0:T(8,128)S(1)}, u32[]{:S(2)}, u32[]{:S(2)}) collective-permute-start(f32[8,432]{1,0:T(8,128)S(1)} %reshape.270), channel_id=1, source_target_pairs={{0,15},{1,0},{2,1},{3,2},{4,3},{5,4},{6,5},{7,6},{8,7},{9,8},{10,9... | collective-permute-start | bytes 41480 | tf_op jit(solution)/shard_map/ppermute | solution.py:236
  30.8 14.6 %collective-permute-start.1 = (f32[8,432]{1,0:T(8,128)S(1)}, f32[8,432]{1,0:T(8,128)S(1)}, u32[]{:S(2)}, u32[]{:S(2)}) collective-permute-start(f32[8,432]{1,0:T(8,128)S(1)} %collective-permute-done), channel_id=1, source_target_pairs={{0,1},{1,2},{2,3},{3,4},{4,5},{5,6},{6,7},{7,8},{8,9},{9,10},{10,1... | collective-permute-start | bytes 41480 | tf_op jit(solution)/shard_map/ppermute | solution.py:234
  31.3 14.1 %copy-start.4 = (bf16[384,576]{0,1:T(8,128)(2,1)S(1)}, bf16[384,576]{0,1:T(8,128)(2,1)}, u32[]{:S(2)}) copy-start(bf16[384,576]{0,1:T(8,128)(2,1)} %param.41) | copy-start | bytes 1327108
  31.3 20.0 %copy-start.30 = (bf16[128,12]{0,1:T(8,128)(2,1)S(1)}, bf16[128,12]{0,1:T(8,128)(2,1)}, u32[]{:S(2)}) copy-start(bf16[128,12]{0,1:T(8,128)(2,1)} %param.43) | copy-start | bytes 9220
  31.3 31.7 %copy-start.43 = (f32[12]{0:T(128)S(1)}, f32[12]{0:T(128)}, u32[]{:S(2)}) copy-start(f32[12]{0:T(128)} %param.44) | copy-start | bytes 148
  45.3 18.2 %copy-start.22 = (f32[8,128]{1,0:T(8,128)}, f32[8,128]{1,0:T(8,128)S(1)}, u32[]{:S(2)}) copy-start(f32[8,128]{1,0:T(8,128)S(1)} %get-tuple-element.610) | copy-start | bytes 12292
  45.3 18.2 %copy-start.39 = (pred[8,128]{1,0:T(8,128)(4,1)}, pred[8,128]{1,0:T(8,128)(4,1)S(1)}, u32[]{:S(2)}) copy-start(pred[8,128]{1,0:T(8,128)(4,1)S(1)} %get-tuple-element.667) | copy-start | bytes 3076
  45.3 5.9 %collective-permute-start.2 = (f32[8,432]{1,0:T(8,128)S(1)}, f32[8,432]{1,0:T(8,128)S(1)}, u32[]{:S(2)}, u32[]{:S(2)}) collective-permute-start(f32[8,432]{1,0:T(8,128)S(1)} %collective-permute-done.1), channel_id=1, source_target_pairs={{0,1},{1,2},{2,3},{3,4},{4,5},{5,6},{6,7},{7,8},{8,9},{9,10},{10,1... | collective-permute-start | bytes 41480 | tf_op jit(solution)/shard_map/ppermute | solution.py:234
  45.6 6.4 %collective-permute-start.9 = (f32[8,432]{1,0:T(8,128)S(1)}, f32[8,432]{1,0:T(8,128)S(1)}, u32[]{:S(2)}, u32[]{:S(2)}) collective-permute-start(f32[8,432]{1,0:T(8,128)S(1)} %collective-permute-done.8), channel_id=1, source_target_pairs={{0,15},{1,0},{2,1},{3,2},{4,3},{5,4},{6,5},{7,6},{8,7},{9,8},{10,9... | collective-permute-start | bytes 41480 | tf_op jit(solution)/shard_map/ppermute | solution.py:236
  51.3 5.9 %collective-permute-start.3 = (f32[8,432]{1,0:T(8,128)S(1)}, f32[8,432]{1,0:T(8,128)S(1)}, u32[]{:S(2)}, u32[]{:S(2)}) collective-permute-start(f32[8,432]{1,0:T(8,128)S(1)} %collective-permute-done.2), channel_id=1, source_target_pairs={{0,1},{1,2},{2,3},{3,4},{4,5},{5,6},{6,7},{7,8},{8,9},{9,10},{10,1... | collective-permute-start | bytes 41480 | tf_op jit(solution)/shard_map/ppermute | solution.py:234
  52.0 5.9 %collective-permute-start.10 = (f32[8,432]{1,0:T(8,128)S(1)}, f32[8,432]{1,0:T(8,128)S(1)}, u32[]{:S(2)}, u32[]{:S(2)}) collective-permute-start(f32[8,432]{1,0:T(8,128)S(1)} %collective-permute-done.9), channel_id=1, source_target_pairs={{0,15},{1,0},{2,1},{3,2},{4,3},{5,4},{6,5},{7,6},{8,7},{9,8},{10,9... | collective-permute-start | bytes 41480 | tf_op jit(solution)/shard_map/ppermute | solution.py:236
  57.1 5.9 %collective-permute-start.4 = (f32[8,432]{1,0:T(8,128)S(1)}, f32[8,432]{1,0:T(8,128)S(1)}, u32[]{:S(2)}, u32[]{:S(2)}) collective-permute-start(f32[8,432]{1,0:T(8,128)S(1)} %collective-permute-done.3), channel_id=1, source_target_pairs={{0,1},{1,2},{2,3},{3,4},{4,5},{5,6},{6,7},{7,8},{8,9},{9,10},{10,1... | collective-permute-start | bytes 41480 | tf_op jit(solution)/shard_map/ppermute | solution.py:234
  57.9 5.9 %collective-permute-start.11 = (f32[8,432]{1,0:T(8,128)S(1)}, f32[8,432]{1,0:T(8,128)S(1)}, u32[]{:S(2)}, u32[]{:S(2)}) collective-permute-start(f32[8,432]{1,0:T(8,128)S(1)} %collective-permute-done.10), channel_id=1, source_target_pairs={{0,15},{1,0},{2,1},{3,2},{4,3},{5,4},{6,5},{7,6},{8,7},{9,8},{10,9... | collective-permute-start | bytes 41480 | tf_op jit(solution)/shard_map/ppermute | solution.py:236
  63.0 5.9 %collective-permute-start.5 = (f32[8,432]{1,0:T(8,128)S(1)}, f32[8,432]{1,0:T(8,128)S(1)}, u32[]{:S(2)}, u32[]{:S(2)}) collective-permute-start(f32[8,432]{1,0:T(8,128)S(1)} %collective-permute-done.4), channel_id=1, source_target_pairs={{0,1},{1,2},{2,3},{3,4},{4,5},{5,6},{6,7},{7,8},{8,9},{9,10},{10,1... | collective-permute-start | bytes 41480 | tf_op jit(solution)/shard_map/ppermute | solution.py:234
  63.8 5.9 %collective-permute-start.12 = (f32[8,432]{1,0:T(8,128)S(1)}, f32[8,432]{1,0:T(8,128)S(1)}, u32[]{:S(2)}, u32[]{:S(2)}) collective-permute-start(f32[8,432]{1,0:T(8,128)S(1)} %collective-permute-done.11), channel_id=1, source_target_pairs={{0,15},{1,0},{2,1},{3,2},{4,3},{5,4},{6,5},{7,6},{8,7},{9,8},{10,9... | collective-permute-start | bytes 41480 | tf_op jit(solution)/shard_map/ppermute | solution.py:236
  68.8 5.9 %collective-permute-start.6 = (f32[8,432]{1,0:T(8,128)S(1)}, f32[8,432]{1,0:T(8,128)S(1)}, u32[]{:S(2)}, u32[]{:S(2)}) collective-permute-start(f32[8,432]{1,0:T(8,128)S(1)} %collective-permute-done.5), channel_id=1, source_target_pairs={{0,1},{1,2},{2,3},{3,4},{4,5},{5,6},{6,7},{7,8},{8,9},{9,10},{10,1... | collective-permute-start | bytes 41480 | tf_op jit(solution)/shard_map/ppermute | solution.py:234
  69.1 28.2 %copy-start.35 = (f32[12]{0:T(128)S(1)}, f32[12]{0:T(128)}, u32[]{:S(2)}) copy-start(f32[12]{0:T(128)} %broadcast_multiply_fusion.5) | copy-start | bytes 148
  69.7 24.7 %collective-permute-start.13 = (f32[8,432]{1,0:T(8,128)S(1)}, f32[8,432]{1,0:T(8,128)S(1)}, u32[]{:S(2)}, u32[]{:S(2)}) collective-permute-start(f32[8,432]{1,0:T(8,128)S(1)} %collective-permute-done.12), channel_id=1, source_target_pairs={{0,15},{1,0},{2,1},{3,2},{4,3},{5,4},{6,5},{7,6},{8,7},{9,8},{10,9... | collective-permute-start | bytes 41480 | tf_op jit(solution)/shard_map/ppermute | solution.py:236
  74.7 20.9 %collective-permute-start.7 = (f32[8,432]{1,0:T(8,128)S(1)}, f32[8,432]{1,0:T(8,128)S(1)}, u32[]{:S(2)}, u32[]{:S(2)}) collective-permute-start(f32[8,432]{1,0:T(8,128)S(1)} %collective-permute-done.6), channel_id=1, source_target_pairs={{0,1},{1,2},{2,3},{3,4},{4,5},{5,6},{6,7},{7,8},{8,9},{9,10},{10,1... | collective-permute-start | bytes 41480 | tf_op jit(solution)/shard_map/ppermute | solution.py:234
  94.4 2.7 %collective-permute-start.14 = (f32[8,432]{1,0:T(8,128)S(1)}, f32[8,432]{1,0:T(8,128)S(1)}, u32[]{:S(2)}, u32[]{:S(2)}) collective-permute-start(f32[8,432]{1,0:T(8,128)S(1)} %collective-permute-done.13), channel_id=1, source_target_pairs={{0,15},{1,0},{2,1},{3,2},{4,3},{5,4},{6,5},{7,6},{8,7},{9,8},{10,9... | collective-permute-start | bytes 41480 | tf_op jit(solution)/shard_map/ppermute | solution.py:236
  97.3 4.2 %copy-start.25 = (f32[8,3]{0,1:T(4,128)S(1)}, f32[8,3]{0,1:T(4,128)}, u32[]{:S(2)}) copy-start(f32[8,3]{0,1:T(4,128)} %copy-done.24) | copy-start | bytes 292
  97.3 4.3 %copy-start.14 = (f32[8,3,3]{1,2,0:T(4,128)S(1)}, f32[8,3,3]{1,2,0:T(4,128)}, u32[]{:S(2)}) copy-start(f32[8,3,3]{1,2,0:T(4,128)} %copy.80) | copy-start | bytes 868
  97.3 4.8 %copy-start.18 = (f32[8,384]{1,0:T(8,128)S(1)}, f32[8,384]{1,0:T(8,128)}, u32[]{:S(2)}) copy-start(f32[8,384]{1,0:T(8,128)} %param.28) | copy-start | bytes 36868
  99.9 4.9 %copy-start.3 = (bf16[384,576]{0,1:T(8,128)(2,1)S(1)}, bf16[384,576]{0,1:T(8,128)(2,1)}, u32[]{:S(2)}) copy-start(bf16[384,576]{0,1:T(8,128)(2,1)} %param.42) | copy-start | bytes 1327108
  100.3 4.9 %copy-start.11 = (f32[8,3,3]{2,1,0:T(4,128)S(1)}, f32[8,3,3]{2,1,0:T(4,128)}, u32[]{:S(2)}) copy-start(f32[8,3,3]{2,1,0:T(4,128)} %copy-done.10) | copy-start | bytes 868
  100.4 5.2 %copy-start.13 = (f32[8,3,3]{0,2,1:T(4,128)S(1)}, f32[8,3,3]{0,2,1:T(4,128)}, u32[]{:S(2)}) copy-start(f32[8,3,3]{0,2,1:T(4,128)} %copy-done.12) | copy-start | bytes 868
  102.2 10.7 %copy-start.7 = (bf16[384,128]{1,0:T(8,128)(2,1)S(1)}, bf16[384,128]{1,0:T(8,128)(2,1)}, u32[]{:S(2)}) copy-start(bf16[384,128]{1,0:T(8,128)(2,1)} %param.34) | copy-start | bytes 294916
  102.6 35.6 %copy-start.16 = (f32[128]{0:T(128)S(1)}, f32[128]{0:T(128)}, u32[]{:S(2)}) copy-start(f32[128]{0:T(128)} %param.37) | copy-start | bytes 1540
  107.0 5.9 %collective-permute-start.15 = (f32[8,432]{1,0:T(8,128)S(1)}, f32[8,432]{1,0:T(8,128)S(1)}, u32[]{:S(2)}, u32[]{:S(2)}) collective-permute-start(f32[8,432]{1,0:T(8,128)S(1)} %reshape.281), channel_id=1, source_target_pairs={{0,1},{1,2},{2,3},{3,4},{4,5},{5,6},{6,7},{7,8},{8,9},{9,10},{10,1... | collective-permute-start | bytes 41480 | tf_op jit(solution)/shard_map/ppermute | solution.py:234
  107.7 29.2 %collective-permute-start.23 = (f32[8,432]{1,0:T(8,128)S(1)}, f32[8,432]{1,0:T(8,128)S(1)}, u32[]{:S(2)}, u32[]{:S(2)}) collective-permute-start(f32[8,432]{1,0:T(8,128)S(1)} %reshape.281), channel_id=1, source_target_pairs={{0,15},{1,0},{2,1},{3,2},{4,3},{5,4},{6,5},{7,6},{8,7},{9,8},{10,9... | collective-permute-start | bytes 41480 | tf_op jit(solution)/shard_map/ppermute | solution.py:236
  112.9 5.9 %copy-start.28 = (f32[8,432]{1,0:T(8,128)}, f32[8,432]{1,0:T(8,128)S(1)}, u32[]{:S(2)}) copy-start(f32[8,432]{1,0:T(8,128)S(1)} %collective-permute-done.15) | copy-start | bytes 41476
  112.9 5.9 %collective-permute-start.16 = (f32[8,432]{1,0:T(8,128)S(1)}, f32[8,432]{1,0:T(8,128)S(1)}, u32[]{:S(2)}, u32[]{:S(2)}) collective-permute-start(f32[8,432]{1,0:T(8,128)S(1)} %collective-permute-done.15), channel_id=1, source_target_pairs={{0,1},{1,2},{2,3},{3,4},{4,5},{5,6},{6,7},{7,8},{8,9},{9,10},{10,1... | collective-permute-start | bytes 41480 | tf_op jit(solution)/shard_map/ppermute | solution.py:234
  118.7 19.4 %collective-permute-start.17 = (f32[8,432]{1,0:T(8,128)S(1)}, f32[8,432]{1,0:T(8,128)S(1)}, u32[]{:S(2)}, u32[]{:S(2)}) collective-permute-start(f32[8,432]{1,0:T(8,128)S(1)} %collective-permute-done.16), channel_id=1, source_target_pairs={{0,1},{1,2},{2,3},{3,4},{4,5},{5,6},{6,7},{7,8},{8,9},{9,10},{10,1... | collective-permute-start | bytes 41480 | tf_op jit(solution)/shard_map/ppermute | solution.py:234
  136.9 29.6 %collective-permute-start.24 = (f32[8,432]{1,0:T(8,128)S(1)}, f32[8,432]{1,0:T(8,128)S(1)}, u32[]{:S(2)}, u32[]{:S(2)}) collective-permute-start(f32[8,432]{1,0:T(8,128)S(1)} %collective-permute-done.23), channel_id=1, source_target_pairs={{0,15},{1,0},{2,1},{3,2},{4,3},{5,4},{6,5},{7,6},{8,7},{9,8},{10,9... | collective-permute-start | bytes 41480 | tf_op jit(solution)/shard_map/ppermute | solution.py:236
  138.2 32.9 %collective-permute-start.18 = (f32[8,432]{1,0:T(8,128)S(1)}, f32[8,432]{1,0:T(8,128)S(1)}, u32[]{:S(2)}, u32[]{:S(2)}) collective-permute-start(f32[8,432]{1,0:T(8,128)S(1)} %collective-permute-done.17), channel_id=1, source_target_pairs={{0,1},{1,2},{2,3},{3,4},{4,5},{5,6},{6,7},{7,8},{8,9},{9,10},{10,1... | collective-permute-start | bytes 41480 | tf_op jit(solution)/shard_map/ppermute | solution.py:234
  138.2 38.7 %copy-start.31 = (bf16[128,12]{0,1:T(8,128)(2,1)S(1)}, bf16[128,12]{0,1:T(8,128)(2,1)}, u32[]{:S(2)}) copy-start(bf16[128,12]{0,1:T(8,128)(2,1)} %param.43) | copy-start | bytes 9220
  166.6 42.7 %copy-start.29 = (f32[8,432]{1,0:T(8,128)S(1)}, f32[8,432]{1,0:T(8,128)}, u32[]{:S(2)}) copy-start(f32[8,432]{1,0:T(8,128)} %copy-done.28) | copy-start | bytes 41476
  166.6 42.7 %copy-start.27 = (f32[8,432]{1,0:T(8,128)S(1)}, f32[8,432]{1,0:T(8,128)}, u32[]{:S(2)}) copy-start(f32[8,432]{1,0:T(8,128)} %copy-done.26) | copy-start | bytes 41476
  166.6 5.9 %collective-permute-start.25 = (f32[8,432]{1,0:T(8,128)S(1)}, f32[8,432]{1,0:T(8,128)S(1)}, u32[]{:S(2)}, u32[]{:S(2)}) collective-permute-start(f32[8,432]{1,0:T(8,128)S(1)} %collective-permute-done.24), channel_id=1, source_target_pairs={{0,15},{1,0},{2,1},{3,2},{4,3},{5,4},{6,5},{7,6},{8,7},{9,8},{10,9... | collective-permute-start | bytes 41480 | tf_op jit(solution)/shard_map/ppermute | solution.py:236
  171.1 5.9 %collective-permute-start.19 = (f32[8,432]{1,0:T(8,128)S(1)}, f32[8,432]{1,0:T(8,128)S(1)}, u32[]{:S(2)}, u32[]{:S(2)}) collective-permute-start(f32[8,432]{1,0:T(8,128)S(1)} %collective-permute-done.18), channel_id=1, source_target_pairs={{0,1},{1,2},{2,3},{3,4},{4,5},{5,6},{6,7},{7,8},{8,9},{9,10},{10,1... | collective-permute-start | bytes 41480 | tf_op jit(solution)/shard_map/ppermute | solution.py:234
  172.5 5.9 %collective-permute-start.26 = (f32[8,432]{1,0:T(8,128)S(1)}, f32[8,432]{1,0:T(8,128)S(1)}, u32[]{:S(2)}, u32[]{:S(2)}) collective-permute-start(f32[8,432]{1,0:T(8,128)S(1)} %collective-permute-done.25), channel_id=1, source_target_pairs={{0,15},{1,0},{2,1},{3,2},{4,3},{5,4},{6,5},{7,6},{8,7},{9,8},{10,9... | collective-permute-start | bytes 41480 | tf_op jit(solution)/shard_map/ppermute | solution.py:236
  176.9 5.9 %collective-permute-start.20 = (f32[8,432]{1,0:T(8,128)S(1)}, f32[8,432]{1,0:T(8,128)S(1)}, u32[]{:S(2)}, u32[]{:S(2)}) collective-permute-start(f32[8,432]{1,0:T(8,128)S(1)} %collective-permute-done.19), channel_id=1, source_target_pairs={{0,1},{1,2},{2,3},{3,4},{4,5},{5,6},{6,7},{7,8},{8,9},{9,10},{10,1... | collective-permute-start | bytes 41480 | tf_op jit(solution)/shard_map/ppermute | solution.py:234
  178.4 5.9 %collective-permute-start.27 = (f32[8,432]{1,0:T(8,128)S(1)}, f32[8,432]{1,0:T(8,128)S(1)}, u32[]{:S(2)}, u32[]{:S(2)}) collective-permute-start(f32[8,432]{1,0:T(8,128)S(1)} %collective-permute-done.26), channel_id=1, source_target_pairs={{0,15},{1,0},{2,1},{3,2},{4,3},{5,4},{6,5},{7,6},{8,7},{9,8},{10,9... | collective-permute-start | bytes 41480 | tf_op jit(solution)/shard_map/ppermute | solution.py:236
  182.8 5.9 %collective-permute-start.21 = (f32[8,432]{1,0:T(8,128)S(1)}, f32[8,432]{1,0:T(8,128)S(1)}, u32[]{:S(2)}, u32[]{:S(2)}) collective-permute-start(f32[8,432]{1,0:T(8,128)S(1)} %collective-permute-done.20), channel_id=1, source_target_pairs={{0,1},{1,2},{2,3},{3,4},{4,5},{5,6},{6,7},{7,8},{8,9},{9,10},{10,1... | collective-permute-start | bytes 41480 | tf_op jit(solution)/shard_map/ppermute | solution.py:234
  183.0 27.9 %copy-start.36 = (f32[12]{0:T(128)S(1)}, f32[12]{0:T(128)}, u32[]{:S(2)}) copy-start(f32[12]{0:T(128)} %broadcast_multiply_fusion.5) | copy-start | bytes 148
  184.2 23.6 %collective-permute-start.28 = (f32[8,432]{1,0:T(8,128)S(1)}, f32[8,432]{1,0:T(8,128)S(1)}, u32[]{:S(2)}, u32[]{:S(2)}) collective-permute-start(f32[8,432]{1,0:T(8,128)S(1)} %collective-permute-done.27), channel_id=1, source_target_pairs={{0,15},{1,0},{2,1},{3,2},{4,3},{5,4},{6,5},{7,6},{8,7},{9,8},{10,9... | collective-permute-start | bytes 41480 | tf_op jit(solution)/shard_map/ppermute | solution.py:236
  188.7 20.5 %collective-permute-start.22 = (f32[8,432]{1,0:T(8,128)S(1)}, f32[8,432]{1,0:T(8,128)S(1)}, u32[]{:S(2)}, u32[]{:S(2)}) collective-permute-start(f32[8,432]{1,0:T(8,128)S(1)} %collective-permute-done.21), channel_id=1, source_target_pairs={{0,1},{1,2},{2,3},{3,4},{4,5},{5,6},{6,7},{7,8},{8,9},{9,10},{10,1... | collective-permute-start | bytes 41480 | tf_op jit(solution)/shard_map/ppermute | solution.py:234
  206.9 4.3 %copy-start.44 = (pred[128]{0:T(512)(128)(4,1)S(1)}, pred[128]{0:T(512)(128)(4,1)}, u32[]{:S(2)}) copy-start(pred[128]{0:T(512)(128)(4,1)} %broadcast_compare_fusion.1) | copy-start | bytes 388
  207.9 2.7 %collective-permute-start.29 = (f32[8,432]{1,0:T(8,128)S(1)}, f32[8,432]{1,0:T(8,128)S(1)}, u32[]{:S(2)}, u32[]{:S(2)}) collective-permute-start(f32[8,432]{1,0:T(8,128)S(1)} %collective-permute-done.28), channel_id=1, source_target_pairs={{0,15},{1,0},{2,1},{3,2},{4,3},{5,4},{6,5},{7,6},{8,7},{9,8},{10,9... | collective-permute-start | bytes 41480 | tf_op jit(solution)/shard_map/ppermute | solution.py:236
  (11 other events, 22.0 us)
